TPU v7x, 128 devices: a whole 4x4x4 slice. The times are simulated.
128 devices in a mesh: seq: 128 (over z, y, x, core).
Axes of the slice: x: 4, y: 4, z: 4, core: 2. Of those that a mesh axis runs over, the one named last changes fastest.
Arguments:
- queries: bfloat16 [32768, 3200], P('seq'), may hold values from -6 to 6
- keys: bfloat16 [32768, 3200], P('seq'), may hold values from -6 to 6
- values: bfloat16 [32768, 3200], P('seq'), may hold values from -6 to 6
- img_height: int32 [1026], replicated, may hold values from 0 to 56, as said below
- img_width: int32 [1026], replicated, may hold values from 0 to 32, as said below
- norm_gain: float32 [12800], replicated, may hold values from 0.5 to 1.5
- norm_bias: float32 [12800], replicated, may hold values from -3 to 3
Outputs:
- merged: bfloat16 [8192, 12800], P('seq')
Inputs may be any that keep to these rules, and one draw needn't show every extreme that they name: Images are packed in slot order without gaps: the products img_height * img_width sum to 32768; heights and widths are even; an image has at most 896 patches and some image has exactly 896; some image is 56 patches high; slots after the last image hold zero rows and zero columns, and there is always at least one such slot. `img_width`: A nonempty image is at most 32 patches wide, and some image is exactly 32 wide.
All inputs are finite; a program needn't handle non-finite values.
Results may differ from a plain program's by a relative error of at most 0.0053.
Values may be sent and summed in bfloat16 or wider, within the bound.
A program may use at most 128 MiB of HBM per device.

v0:
```python
import math

import jax
import jax.numpy as jnp
from jax import lax
from jax.sharding import PartitionSpec as P

HEAD_DIM = 128
WMAX = 32
REACH = 4


def shifted(block, axis, distance):
    devices = range(lax.axis_size(axis))
    route = [(i - distance, i) for i in devices if i - distance in devices]
    return lax.ppermute(block, axis, route)


def extended(block, sides, width):
    for axis, dim in sides:
        count = lax.axis_size(axis)
        forward = [(i, i + 1) for i in range(count - 1)]
        backward = [(target, source) for source, target in forward]
        low = lax.ppermute(
            lax.slice_in_dim(block, block.shape[dim] - width, None, axis=dim), axis, forward
        )
        high = lax.ppermute(lax.slice_in_dim(block, 0, width, axis=dim), axis, backward)
        block = jnp.concatenate([low, block, high], axis=dim)
    return block


def image_index(image_ends, positions):
    return jnp.searchsorted(image_ends, positions, side="right")


def head_attention(query_block, key_window, value_window, allowed):
    softmax_scale = 1.0 / math.sqrt(HEAD_DIM)
    head_count = query_block.shape[1] // HEAD_DIM

    def one_head(head_index, result):
        column = head_index * HEAD_DIM
        q_head = lax.dynamic_slice_in_dim(query_block, column, HEAD_DIM, 1)
        k_head = lax.dynamic_slice_in_dim(key_window, column, HEAD_DIM, 1)
        v_head = lax.dynamic_slice_in_dim(value_window, column, HEAD_DIM, 1)
        scores = (
            lax.dot_general(
                q_head, k_head, (((1,), (1,)), ((), ())), preferred_element_type=jnp.float32
            )
            * softmax_scale
        )
        scores = jnp.where(allowed, scores, -jnp.inf)
        row_max = jnp.max(scores, axis=1, keepdims=True)
        weights = jnp.exp(scores - row_max)
        totals = jnp.sum(weights, axis=1, keepdims=True)
        weights_low = weights.astype(jnp.bfloat16)
        head_out = (
            jnp.dot(weights_low, v_head, preferred_element_type=jnp.float32) / totals
        ).astype(jnp.bfloat16)
        return lax.dynamic_update_slice_in_dim(result, head_out, column, 1)

    start_value = jnp.zeros(query_block.shape, jnp.bfloat16)
    return lax.fori_loop(0, head_count, one_head, start_value)


def layer_norm(features, norm_gain, norm_bias):
    values_wide = features.astype(jnp.float32)
    center = jnp.mean(values_wide, axis=1, keepdims=True)
    spread = jnp.mean(jnp.square(values_wide - center), axis=1, keepdims=True)
    return ((values_wide - center) * lax.rsqrt(spread + 1e-06) * norm_gain + norm_bias).astype(
        jnp.bfloat16
    )


def body(queries, keys, values, img_height, img_width, norm_gain, norm_bias):
    shard_rows = queries.shape[0]
    device = lax.axis_index("seq")
    devices = lax.axis_size("seq")
    lengths = img_height * img_width
    image_ends = jnp.cumsum(lengths)
    starts = image_ends - lengths
    pieces = {}
    for offset in range(-REACH, REACH + 1):
        if offset != 0:
            pieces[offset] = shifted((keys, values), "seq", -offset)
    pieces[0] = (keys, values)
    order = list(range(-REACH, REACH + 1))
    key_window = jnp.concatenate([pieces[offset][0] for offset in order], axis=0)
    value_window = jnp.concatenate([pieces[offset][1] for offset in order], axis=0)
    window_rows = (2 * REACH + 1) * shard_rows
    positions = (device - REACH) * shard_rows + jnp.arange(window_rows, dtype=jnp.int32)
    inside = (positions >= 0) & (positions < devices * shard_rows)
    window_ids = jnp.where(inside, image_index(image_ends, positions), -1)
    query_ids = window_ids[REACH * shard_rows : (REACH + 1) * shard_rows]
    allowed = query_ids[:, None] == window_ids[None, :]
    attention = head_attention(queries, key_window, value_window, allowed)
    padded = extended(attention, (("seq", 0),), WMAX)
    merged_rows = shard_rows // 4
    targets = device * merged_rows + jnp.arange(merged_rows, dtype=jnp.int32)
    owners = image_index(image_ends // 4, targets)
    slot_index = jnp.arange(img_width.shape[0], dtype=jnp.int32)
    select = owners[:, None] == slot_index[None, :]
    first = jnp.sum(jnp.where(select, starts[None, :], 0), axis=1)
    across = jnp.sum(jnp.where(select, img_width[None, :], 0), axis=1)
    within = targets - first // 4
    half_width = across // 2
    grid_row = within // half_width
    grid_col = within - grid_row * half_width
    source = first + 2 * grid_row * across + 2 * grid_col
    local_row = source - (device * shard_rows - WMAX)
    gathered = jnp.concatenate(
        [
            padded[local_row],
            padded[local_row + 1],
            padded[local_row + across],
            padded[local_row + across + 1],
        ],
        axis=1,
    )
    return layer_norm(gathered, norm_gain, norm_bias)


def solution(mesh):
    in_specs = (P("seq", None), P("seq", None), P("seq", None), P(), P(), P(), P())
    out_specs = P("seq", None)
    return jax.shard_map(body, mesh=mesh, in_specs=in_specs, out_specs=out_specs, check_vma=False)
```

profile of v0, /device:TPU:5, one launch (start us, length us, event | category | flops | bytes accessed | tf_op | source)
XLA Modules:
  0.0 576.8 jit_solution(10748182636006307342)
XLA Ops:
  17.2 136.6 %while.63 = (s32[]{:T(128)}, u32[2304]{0:T(1024)S(1)}, u32[2304]{0:T(1024)S(1)}, s32[1026]{0:T(1024)S(1)}, s32[]{:T(128)}, /*index=5*/s32[]{:T(128)}, s32[]{:T(128)}, s32[]{}) while((s32[]{:T(128)}, u32[2304]{0:T(1024)S(1)}, u32[2304]{0:T(1024)S(1)}, s32[1026]{0:T(1024)S(1)}, s32[]{:T(128)}, /*index=5*/s32[]{:T(128)}, s32[]{:T(128)}, ...), condition=%wide.region_3.4_spmd.clone, body=%wide.region_2.3_spmd.clone.sunk | while | flops 46852 | bytes 164465 | solution.py:33
  17.3 12.3 %gather_fusion = s32[2304]{0:T(1024)S(1)} fusion(s32[1026]{0:T(1024)S(1)} %get-tuple-element.499, u32[3072]{0:T(1024)S(1)} %pad_clamp_fusion.8), kind=kCustom, calls=%fused_computation.clone.clone.1 | custom fusion | bytes 27648 | tf_op jit(solution)/shard_map/jit(searchsorted)/jit(_searchsorted_scan_impl)/vmap(jit(_searchsorted_scan_impl))/while/body/eval_jaxpr/gather | solution.py:33
  29.7 12.3 %gather_fusion = s32[2304]{0:T(1024)S(1)} fusion(s32[1026]{0:T(1024)S(1)} %get-tuple-element.499, u32[3072]{0:T(1024)S(1)} %pad_clamp_fusion.8), kind=kCustom, calls=%fused_computation.clone.clone.1 | custom fusion | bytes 27648 | tf_op jit(solution)/shard_map/jit(searchsorted)/jit(_searchsorted_scan_impl)/vmap(jit(_searchsorted_scan_impl))/while/body/eval_jaxpr/gather | solution.py:33
  42.1 12.3 %gather_fusion = s32[2304]{0:T(1024)S(1)} fusion(s32[1026]{0:T(1024)S(1)} %get-tuple-element.499, u32[3072]{0:T(1024)S(1)} %pad_clamp_fusion.8), kind=kCustom, calls=%fused_computation.clone.clone.1 | custom fusion | bytes 27648 | tf_op jit(solution)/shard_map/jit(searchsorted)/jit(_searchsorted_scan_impl)/vmap(jit(_searchsorted_scan_impl))/while/body/eval_jaxpr/gather | solution.py:33
  54.5 12.3 %gather_fusion = s32[2304]{0:T(1024)S(1)} fusion(s32[1026]{0:T(1024)S(1)} %get-tuple-element.499, u32[3072]{0:T(1024)S(1)} %pad_clamp_fusion.8), kind=kCustom, calls=%fused_computation.clone.clone.1 | custom fusion | bytes 27648 | tf_op jit(solution)/shard_map/jit(searchsorted)/jit(_searchsorted_scan_impl)/vmap(jit(_searchsorted_scan_impl))/while/body/eval_jaxpr/gather | solution.py:33
  66.9 12.3 %gather_fusion = s32[2304]{0:T(1024)S(1)} fusion(s32[1026]{0:T(1024)S(1)} %get-tuple-element.499, u32[3072]{0:T(1024)S(1)} %pad_clamp_fusion.8), kind=kCustom, calls=%fused_computation.clone.clone.1 | custom fusion | bytes 27648 | tf_op jit(solution)/shard_map/jit(searchsorted)/jit(_searchsorted_scan_impl)/vmap(jit(_searchsorted_scan_impl))/while/body/eval_jaxpr/gather | solution.py:33
  79.3 12.3 %gather_fusion = s32[2304]{0:T(1024)S(1)} fusion(s32[1026]{0:T(1024)S(1)} %get-tuple-element.499, u32[3072]{0:T(1024)S(1)} %pad_clamp_fusion.8), kind=kCustom, calls=%fused_computation.clone.clone.1 | custom fusion | bytes 27648 | tf_op jit(solution)/shard_map/jit(searchsorted)/jit(_searchsorted_scan_impl)/vmap(jit(_searchsorted_scan_impl))/while/body/eval_jaxpr/gather | solution.py:33
  91.8 12.3 %gather_fusion = s32[2304]{0:T(1024)S(1)} fusion(s32[1026]{0:T(1024)S(1)} %get-tuple-element.499, u32[3072]{0:T(1024)S(1)} %pad_clamp_fusion.8), kind=kCustom, calls=%fused_computation.clone.clone.1 | custom fusion | bytes 27648 | tf_op jit(solution)/shard_map/jit(searchsorted)/jit(_searchsorted_scan_impl)/vmap(jit(_searchsorted_scan_impl))/while/body/eval_jaxpr/gather | solution.py:33
  104.2 12.3 %gather_fusion = s32[2304]{0:T(1024)S(1)} fusion(s32[1026]{0:T(1024)S(1)} %get-tuple-element.499, u32[3072]{0:T(1024)S(1)} %pad_clamp_fusion.8), kind=kCustom, calls=%fused_computation.clone.clone.1 | custom fusion | bytes 27648 | tf_op jit(solution)/shard_map/jit(searchsorted)/jit(_searchsorted_scan_impl)/vmap(jit(_searchsorted_scan_impl))/while/body/eval_jaxpr/gather | solution.py:33
  116.6 12.3 %gather_fusion = s32[2304]{0:T(1024)S(1)} fusion(s32[1026]{0:T(1024)S(1)} %get-tuple-element.499, u32[3072]{0:T(1024)S(1)} %pad_clamp_fusion.8), kind=kCustom, calls=%fused_computation.clone.clone.1 | custom fusion | bytes 27648 | tf_op jit(solution)/shard_map/jit(searchsorted)/jit(_searchsorted_scan_impl)/vmap(jit(_searchsorted_scan_impl))/while/body/eval_jaxpr/gather | solution.py:33
  129.0 12.3 %gather_fusion = s32[2304]{0:T(1024)S(1)} fusion(s32[1026]{0:T(1024)S(1)} %get-tuple-element.499, u32[3072]{0:T(1024)S(1)} %pad_clamp_fusion.8), kind=kCustom, calls=%fused_computation.clone.clone.1 | custom fusion | bytes 27648 | tf_op jit(solution)/shard_map/jit(searchsorted)/jit(_searchsorted_scan_impl)/vmap(jit(_searchsorted_scan_impl))/while/body/eval_jaxpr/gather | solution.py:33
  141.4 12.3 %gather_fusion = s32[2304]{0:T(1024)S(1)} fusion(s32[1026]{0:T(1024)S(1)} %get-tuple-element.499, u32[3072]{0:T(1024)S(1)} %pad_clamp_fusion.8), kind=kCustom, calls=%fused_computation.clone.clone.1 | custom fusion | bytes 27648 | tf_op jit(solution)/shard_map/jit(searchsorted)/jit(_searchsorted_scan_impl)/vmap(jit(_searchsorted_scan_impl))/while/body/eval_jaxpr/gather | solution.py:33
  153.8 9.1 %while.64 = (s32[]{:T(128)}, u32[64]{0:T(128)S(1)}, u32[64]{0:T(128)S(1)}, s32[1026]{0:T(1024)S(1)}, s32[]{:T(128)}, /*index=5*/s32[]{:T(128)}, s32[]{:T(128)}, s32[]{}) while((s32[]{:T(128)}, u32[64]{0:T(128)S(1)}, u32[64]{0:T(128)S(1)}, s32[1026]{0:T(1024)S(1)}, s32[]{:T(128)}, /*index=5*/s32[]{:T(128)}, s32[]{:T(128)}, ...), condition=%wide.region_9.10_spmd.clone, body=%wide.region_8.9_spmd.clone.sunk | while | flops 1924 | bytes 7280 | solution.py:33
  168.4 5.6 collective-permute-start.9
  184.3 18.8 %collective-permute-done.8 = bf16[256,3200]{1,0:T(8,128)(2,1)S(1)} collective-permute-done((bf16[256,3200]{1,0:T(8,128)(2,1)S(1)}, bf16[256,3200]{1,0:T(8,128)(2,1)S(1)}, u32[]{:S(2)}, u32[]{:S(2)}) %collective-permute-start.8) | collective-permute-done | bytes 1638432 | tf_op jit(solution)/shard_map/ppermute | solution.py:16
  205.2 51.7 %collective-permute-done.9 = bf16[256,3200]{1,0:T(8,128)(2,1)S(1)} collective-permute-done((bf16[256,3200]{1,0:T(8,128)(2,1)S(1)}, bf16[256,3200]{1,0:T(8,128)(2,1)S(1)}, u32[]{:S(2)}, u32[]{:S(2)}) %collective-permute-start.9) | collective-permute-done | bytes 1638432 | tf_op jit(solution)/shard_map/ppermute | solution.py:16
  259.0 11.0 %collective-permute-done.10 = bf16[256,3200]{1,0:T(8,128)(2,1)S(1)} collective-permute-done((bf16[256,3200]{1,0:T(8,128)(2,1)S(1)}, bf16[256,3200]{1,0:T(8,128)(2,1)S(1)}, u32[]{:S(2)}, u32[]{:S(2)}) %collective-permute-start.10) | collective-permute-done | bytes 1638432 | tf_op jit(solution)/shard_map/ppermute | solution.py:16
  274.7 30.3 %collective-permute-done.11 = bf16[256,3200]{1,0:T(8,128)(2,1)S(1)} collective-permute-done((bf16[256,3200]{1,0:T(8,128)(2,1)S(1)}, bf16[256,3200]{1,0:T(8,128)(2,1)S(1)}, u32[]{:S(2)}, u32[]{:S(2)}) %collective-permute-start.11) | collective-permute-done | bytes 1638432 | tf_op jit(solution)/shard_map/ppermute | solution.py:16
  311.8 9.2 %collective-permute-done.6 = bf16[256,3200]{1,0:T(8,128)(2,1)S(1)} collective-permute-done((bf16[256,3200]{1,0:T(8,128)(2,1)S(1)}, bf16[256,3200]{1,0:T(8,128)(2,1)S(1)}, u32[]{:S(2)}, u32[]{:S(2)}) %collective-permute-start.6) | collective-permute-done | bytes 1638432 | tf_op jit(solution)/shard_map/ppermute | solution.py:16
  323.1 20.9 %collective-permute-done.7 = bf16[256,3200]{1,0:T(8,128)(2,1)S(1)} collective-permute-done((bf16[256,3200]{1,0:T(8,128)(2,1)S(1)}, bf16[256,3200]{1,0:T(8,128)(2,1)S(1)}, u32[]{:S(2)}, u32[]{:S(2)}) %collective-permute-start.7) | collective-permute-done | bytes 1638432 | tf_op jit(solution)/shard_map/ppermute | solution.py:16
  344.2 33.5 %collective-permute-done.12 = bf16[256,3200]{1,0:T(8,128)(2,1)S(1)} collective-permute-done((bf16[256,3200]{1,0:T(8,128)(2,1)S(1)}, bf16[256,3200]{1,0:T(8,128)(2,1)S(1)}, u32[]{:S(2)}, u32[]{:S(2)}) %collective-permute-start.12) | collective-permute-done | bytes 1638432 | tf_op jit(solution)/shard_map/ppermute | solution.py:16
  378.1 74.1 %collective-permute-done.14 = bf16[256,3200]{1,0:T(8,128)(2,1)S(1)} collective-permute-done((bf16[256,3200]{1,0:T(8,128)(2,1)S(1)}, bf16[256,3200]{1,0:T(8,128)(2,1)S(1)}, u32[]{:S(2)}, u32[]{:S(2)}) %collective-permute-start.14) | collective-permute-done | bytes 1638432 | tf_op jit(solution)/shard_map/ppermute | solution.py:16
  457.8 96.6 %while.62 = (s32[]{:T(128)}, bf16[256,3200]{1,0:T(8,128)(2,1)S(1)}, bf16[256,3200]{1,0:T(8,128)(2,1)}, bf16[2304,3200]{1,0:T(8,128)(2,1)}, bf16[2304,3200]{1,0:T...) while((s32[]{:T(128)}, bf16[256,3200]{1,0:T(8,128)(2,1)S(1)}, ...), condition=%wide.region_7.8_spmd.clone, body=%wide.region_4.7_spmd.clone.sunk | while | flops 306773504 | bytes 8406171 | solution.py:62
  554.4 6.3 %collective-permute-start.16 = (bf16[32,3200]{1,0:T(8,128)(2,1)S(1)}, bf16[32,3200]{1,0:T(8,128)(2,1)S(1)}, u32[]{:S(2)}, u32[]{:S(2)}) collective-permute-start(bf16[32,3200]{1,0:T(8,128)(2,1)S(1)} %get-tuple-element.352), channel_id=1, source_target_pairs={{0,1},{1,2},{2,3},{3,4},{4,5},{5,6},{6,7},{7,8},{8,9},{9,10},{10,1... | collective-permute-start | bytes 614408 | tf_op jit(solution)/shard_map/ppermute | solution.py:24
  (270 shorter events, 178.1 us)
Async XLA Ops:
  0.0 163.3 %collective-permute-start = (bf16[256,3200]{1,0:T(8,128)(2,1)}, bf16[256,3200]{1,0:T(8,128)(2,1)}, u32[]{:S(2)}, u32[]{:S(2)}) collective-permute-start(bf16[256,3200]{1,0:T(8,128)(2,1)} %param.14), channel_id=1, source_target_pairs={{0,4},{1,5},{2,6},{3,7},{4,8},{5,9},{6,10},{7,11},{8,12},{9,13},{1... | collective-permute-start | bytes 4915208 | tf_op jit(solution)/shard_map/ppermute | solution.py:16
  3.1 165.2 %collective-permute-start.1 = (bf16[256,3200]{1,0:T(8,128)(2,1)}, bf16[256,3200]{1,0:T(8,128)(2,1)}, u32[]{:S(2)}, u32[]{:S(2)}) collective-permute-start(bf16[256,3200]{1,0:T(8,128)(2,1)} %param.14), channel_id=1, source_target_pairs={{0,3},{1,4},{2,5},{3,6},{4,7},{5,8},{6,9},{7,10},{8,11},{9,12},{10... | collective-permute-start | bytes 4915208 | tf_op jit(solution)/shard_map/ppermute | solution.py:16
  8.7 166.9 %collective-permute-start.2 = (bf16[256,3200]{1,0:T(8,128)(2,1)}, bf16[256,3200]{1,0:T(8,128)(2,1)}, u32[]{:S(2)}, u32[]{:S(2)}) collective-permute-start(bf16[256,3200]{1,0:T(8,128)(2,1)} %param.14), channel_id=1, source_target_pairs={{0,2},{1,3},{2,4},{3,5},{4,6},{5,7},{6,8},{7,9},{8,10},{9,11},{10,... | collective-permute-start | bytes 4915208 | tf_op jit(solution)/shard_map/ppermute | solution.py:16
  11.5 168.3 %collective-permute-start.3 = (bf16[256,3200]{1,0:T(8,128)(2,1)}, bf16[256,3200]{1,0:T(8,128)(2,1)}, u32[]{:S(2)}, u32[]{:S(2)}) collective-permute-start(bf16[256,3200]{1,0:T(8,128)(2,1)} %param.14), channel_id=1, source_target_pairs={{0,1},{1,2},{2,3},{3,4},{4,5},{5,6},{6,7},{7,8},{8,9},{9,10},{10,1... | collective-permute-start | bytes 4915208 | tf_op jit(solution)/shard_map/ppermute | solution.py:16
  13.7 293.8 %collective-permute-start.4 = (bf16[256,3200]{1,0:T(8,128)(2,1)}, bf16[256,3200]{1,0:T(8,128)(2,1)S(1)}, u32[]{:S(2)}, u32[]{:S(2)}) collective-permute-start(bf16[256,3200]{1,0:T(8,128)(2,1)} %param.14), channel_id=1, source_target_pairs={{1,0},{2,1},{3,2},{4,3},{5,4},{6,5},{7,6},{8,7},{9,8},{10,9},{11,1... | collective-permute-start | bytes 4915208 | tf_op jit(solution)/shard_map/ppermute | solution.py:16
  17.2 146.1 %copy-start.3 = (bf16[256,3200]{1,0:T(8,128)(2,1)S(1)}, bf16[256,3200]{1,0:T(8,128)(2,1)}, u32[]{:S(2)}) copy-start(bf16[256,3200]{1,0:T(8,128)(2,1)} %param.15) | copy-start | bytes 4915204
  153.8 9.2 %copy-start.8 = (s32[1026]{0:T(1024)S(1)}, s32[1026]{0:T(1024)}, u32[]{:S(2)}) copy-start(s32[1026]{0:T(1024)} %param.17) | copy-start | bytes 12316
  163.4 39.8 %collective-permute-start.8 = (bf16[256,3200]{1,0:T(8,128)(2,1)S(1)}, bf16[256,3200]{1,0:T(8,128)(2,1)S(1)}, u32[]{:S(2)}, u32[]{:S(2)}) collective-permute-start(bf16[256,3200]{1,0:T(8,128)(2,1)S(1)} %copy-done.3), channel_id=1, source_target_pairs={{0,4},{1,5},{2,6},{3,7},{4,8},{5,9},{6,10},{7,11},{8,12},{9,13},{1... | collective-permute-start | bytes 4915208 | tf_op jit(solution)/shard_map/ppermute | solution.py:16
  168.4 88.5 %collective-permute-start.9 = (bf16[256,3200]{1,0:T(8,128)(2,1)S(1)}, bf16[256,3200]{1,0:T(8,128)(2,1)S(1)}, u32[]{:S(2)}, u32[]{:S(2)}) collective-permute-start(bf16[256,3200]{1,0:T(8,128)(2,1)S(1)} %copy-done.3), channel_id=1, source_target_pairs={{0,3},{1,4},{2,5},{3,6},{4,7},{5,8},{6,9},{7,10},{8,11},{9,12},{10... | collective-permute-start | bytes 4915208 | tf_op jit(solution)/shard_map/ppermute | solution.py:16
  175.6 94.3 %collective-permute-start.10 = (bf16[256,3200]{1,0:T(8,128)(2,1)S(1)}, bf16[256,3200]{1,0:T(8,128)(2,1)S(1)}, u32[]{:S(2)}, u32[]{:S(2)}) collective-permute-start(bf16[256,3200]{1,0:T(8,128)(2,1)S(1)} %copy-done.3), channel_id=1, source_target_pairs={{0,2},{1,3},{2,4},{3,5},{4,6},{5,7},{6,8},{7,9},{8,10},{9,11},{10,... | collective-permute-start | bytes 4915208 | tf_op jit(solution)/shard_map/ppermute | solution.py:16
  179.7 4.3 copy-start.2
  179.8 125.3 %collective-permute-start.11 = (bf16[256,3200]{1,0:T(8,128)(2,1)S(1)}, bf16[256,3200]{1,0:T(8,128)(2,1)S(1)}, u32[]{:S(2)}, u32[]{:S(2)}) collective-permute-start(bf16[256,3200]{1,0:T(8,128)(2,1)S(1)} %copy-done.3), channel_id=1, source_target_pairs={{0,1},{1,2},{2,3},{3,4},{4,5},{5,6},{6,7},{7,8},{8,9},{9,10},{10,1... | collective-permute-start | bytes 4915208 | tf_op jit(solution)/shard_map/ppermute | solution.py:16
  203.1 106.5 %collective-permute-start.5 = (bf16[256,3200]{1,0:T(8,128)(2,1)S(1)}, bf16[256,3200]{1,0:T(8,128)(2,1)S(1)}, u32[]{:S(2)}, u32[]{:S(2)}) collective-permute-start(bf16[256,3200]{1,0:T(8,128)(2,1)S(1)} %copy-done.2), channel_id=1, source_target_pairs={{2,0},{3,1},{4,2},{5,3},{6,4},{7,5},{8,6},{9,7},{10,8},{11,9},{12,... | collective-permute-start | bytes 4915208 | tf_op jit(solution)/shard_map/ppermute | solution.py:16
  256.9 64.1 %collective-permute-start.6 = (bf16[256,3200]{1,0:T(8,128)(2,1)S(1)}, bf16[256,3200]{1,0:T(8,128)(2,1)S(1)}, u32[]{:S(2)}, u32[]{:S(2)}) collective-permute-start(bf16[256,3200]{1,0:T(8,128)(2,1)S(1)} %copy-done.2), channel_id=1, source_target_pairs={{3,0},{4,1},{5,2},{6,3},{7,4},{8,5},{9,6},{10,7},{11,8},{12,9},{13... | collective-permute-start | bytes 4915208 | tf_op jit(solution)/shard_map/ppermute | solution.py:16
  270.0 74.0 %collective-permute-start.7 = (bf16[256,3200]{1,0:T(8,128)(2,1)S(1)}, bf16[256,3200]{1,0:T(8,128)(2,1)S(1)}, u32[]{:S(2)}, u32[]{:S(2)}) collective-permute-start(bf16[256,3200]{1,0:T(8,128)(2,1)S(1)} %copy-done.2), channel_id=1, source_target_pairs={{4,0},{5,1},{6,2},{7,3},{8,4},{9,5},{10,6},{11,7},{12,8},{13,9},{1... | collective-permute-start | bytes 4915208 | tf_op jit(solution)/shard_map/ppermute | solution.py:16
  305.1 72.6 %collective-permute-start.12 = (bf16[256,3200]{1,0:T(8,128)(2,1)S(1)}, bf16[256,3200]{1,0:T(8,128)(2,1)S(1)}, u32[]{:S(2)}, u32[]{:S(2)}) collective-permute-start(bf16[256,3200]{1,0:T(8,128)(2,1)S(1)} %copy-done.3), channel_id=1, source_target_pairs={{1,0},{2,1},{3,2},{4,3},{5,4},{6,5},{7,6},{8,7},{9,8},{10,9},{11,1... | collective-permute-start | bytes 4915208 | tf_op jit(solution)/shard_map/ppermute | solution.py:16
  307.4 70.4 %collective-permute-start.13 = (bf16[256,3200]{1,0:T(8,128)(2,1)S(1)}, bf16[256,3200]{1,0:T(8,128)(2,1)S(1)}, u32[]{:S(2)}, u32[]{:S(2)}) collective-permute-start(bf16[256,3200]{1,0:T(8,128)(2,1)S(1)} %copy-done.3), channel_id=1, source_target_pairs={{2,0},{3,1},{4,2},{5,3},{6,4},{7,5},{8,6},{9,7},{10,8},{11,9},{12,... | collective-permute-start | bytes 4915208 | tf_op jit(solution)/shard_map/ppermute | solution.py:16
  309.6 142.6 %collective-permute-start.14 = (bf16[256,3200]{1,0:T(8,128)(2,1)S(1)}, bf16[256,3200]{1,0:T(8,128)(2,1)S(1)}, u32[]{:S(2)}, u32[]{:S(2)}) collective-permute-start(bf16[256,3200]{1,0:T(8,128)(2,1)S(1)} %copy-done.3), channel_id=1, source_target_pairs={{3,0},{4,1},{5,2},{6,3},{7,4},{8,5},{9,6},{10,7},{11,8},{12,9},{13... | collective-permute-start | bytes 4915208 | tf_op jit(solution)/shard_map/ppermute | solution.py:16
  320.9 131.5 %collective-permute-start.15 = (bf16[256,3200]{1,0:T(8,128)(2,1)S(1)}, bf16[256,3200]{1,0:T(8,128)(2,1)S(1)}, u32[]{:S(2)}, u32[]{:S(2)}) collective-permute-start(bf16[256,3200]{1,0:T(8,128)(2,1)S(1)} %copy-done.3), channel_id=1, source_target_pairs={{4,0},{5,1},{6,2},{7,3},{8,4},{9,5},{10,6},{11,7},{12,8},{13,9},{1... | collective-permute-start | bytes 4915208 | tf_op jit(solution)/shard_map/ppermute | solution.py:16
  344.2 108.6 %copy-start.5 = (bf16[2304,3200]{1,0:T(8,128)(2,1)}, bf16[2304,3200]{1,0:T(8,128)(2,1)S(1)}, u32[]{:S(2)}) copy-start(bf16[2304,3200]{1,0:T(8,128)(2,1)S(1)} %constant_dynamic-update-slice_fusion) | copy-start | bytes 44236804
  452.6 5.2 copy-start.4
  554.4 8.5 %copy-start = (bf16[256,3200]{1,0:T(8,128)(2,1)}, bf16[256,3200]{1,0:T(8,128)(2,1)S(1)}, u32[]{:S(2)}) copy-start(bf16[256,3200]{1,0:T(8,128)(2,1)S(1)} %get-tuple-element.245) | copy-start | bytes 4915204
  554.4 8.9 %collective-permute-start.16 = (bf16[32,3200]{1,0:T(8,128)(2,1)S(1)}, bf16[32,3200]{1,0:T(8,128)(2,1)S(1)}, u32[]{:S(2)}, u32[]{:S(2)}) collective-permute-start(bf16[32,3200]{1,0:T(8,128)(2,1)S(1)} %get-tuple-element.352), channel_id=1, source_target_pairs={{0,1},{1,2},{2,3},{3,4},{4,5},{5,6},{6,7},{7,8},{8,9},{9,10},{10,1... | collective-permute-start | bytes 614408 | tf_op jit(solution)/shard_map/ppermute | solution.py:24
  560.7 7.1 %collective-permute-start.17 = (bf16[32,3200]{1,0:T(8,128)(2,1)S(1)}, bf16[32,3200]{1,0:T(8,128)(2,1)S(1)}, u32[]{:S(2)}, u32[]{:S(2)}) collective-permute-start(bf16[32,3200]{1,0:T(8,128)(2,1)S(1)} %get-tuple-element.351), channel_id=1, source_target_pairs={{1,0},{2,1},{3,2},{4,3},{5,4},{6,5},{7,6},{8,7},{9,8},{10,9},{11,1... | collective-permute-start | bytes 614408 | tf_op jit(solution)/shard_map/ppermute | solution.py:27
  (3 other events, 9.1 us)
where the time goes:
time: 580 us; the launch traced here: 577 us
  waiting for transfers between devices  253 us (44%)
  local copies, waits for them, and re-layouts  165 us (28%)
  matrix products  84.2 us (15%)
  starting transfers between devices  54.3 us (9%)
  other arithmetic  18.9 us (3%)
    ppermute x16, waiting for transfers between devices, shifted(): return lax.ppermute(block, axis, route)  249 us
    gather x22, local copies, waits for them, and re-layouts, image_index(): return jnp.searchsorted(image_ends, positions, side='right')  144 us
    ppermute x16, starting transfers between devices, shifted(): return lax.ppermute(block, axis, route)  46 us
    dot_general x25, matrix products, one_head(): lax.dot_general(q_head, k_head, (((1,), (1,)), ((), ())), preferred_eleme...  42.3 us
    dot_general x25, matrix products, one_head(): jnp.dot(weights_low, v_head, preferred_element_type=jnp.float32) / totals  41.9 us
    unnamed x36, local copies, waits for them, and re-layouts  15.8 us
    reduce_sum x25, other arithmetic, one_head(): totals = jnp.sum(weights, axis=1, keepdims=True)  11.9 us
  transfers between devices with their start and end apart: 18, of which 10 were waited for; matrix products, arithmetic and copies ran while one was open for 27% of the time, Pallas kernels for 0%

commit v1 on v0

v1 whole, which is shorter than its diff:
```python
import functools
import math

import jax
import jax.numpy as jnp
from jax import lax
from jax.experimental import pallas as pl
from jax.experimental.pallas import tpu as pltpu
from jax.sharding import PartitionSpec as P

HEAD = 128
MOST = 896
WMAX = 32
GROUP = 8
ROWS = 256
HEADS = 3
WIDE = HEADS * HEAD
EXTRA = GROUP * WIDE
FULL = WIDE + HEAD
SPAN = GROUP * ROWS
KROWS = SPAN + 2 * MOST
QROWS = SPAN + 2 * WMAX
CHUNK = 256
CHUNKS = 10
QUERY_WINDOW = ROWS + 2 * WMAX
MESH = pl.DeviceIdType.MESH
NEG = -1e30
EXP_SCALE = math.log2(math.e) / math.sqrt(HEAD)


def remote(src, dst, send, recv, device):
    return pltpu.make_async_remote_copy(
        src_ref=src,
        dst_ref=dst,
        send_sem=send,
        recv_sem=recv,
        device_id=(device,),
        device_id_type=MESH,
    )


def greet(devices):
    barrier = pltpu.get_barrier_semaphore()
    for device in devices:
        pl.semaphore_signal(barrier, inc=1, device_id=(device,), device_id_type=MESH)
    pl.semaphore_wait(barrier, len(devices))


def head_columns(index):
    return pl.ds(pl.multiple_of(index * WIDE, HEAD), WIDE)


ORDER = (4, 3, 5, 2, 6, 1, 7)
MAIN = pl.ds(0, WIDE)
LAST = pl.ds(WIDE, HEAD)


def spread_kernel(
    count, k_in, v_in, q_in, k_out, v_out, q_out, stage,
    send, recv, send_last, recv_last, load_sem, store_sem,
    halo_send, halo_recv, halo_send_last, halo_recv_last,
):
    me = lax.axis_index("seq")
    j = lax.rem(me, GROUP)
    first = me - j
    above = lax.rem(me + GROUP, count)
    below = lax.rem(me + count - GROUP, count)
    greet([first + lax.rem(j + o, GROUP) for o in ORDER] + [above, below])
    tensors = ((k_in, k_out, MOST), (v_in, v_out, MOST), (q_in, q_out, WMAX))

    def own_rows(base):
        return pl.ds(pl.multiple_of(base + j * ROWS, 32), ROWS)

    def piece(t, o):
        source, target, base = tensors[t]
        to = lax.rem(j + o, GROUP)
        return remote(
            source.at[:, head_columns(to)], target.at[own_rows(base), MAIN],
            send.at[t, o], recv.at[t, j], first + to,
        )

    def piece_last(t):
        source, target, base = tensors[t]
        return remote(
            source.at[:, pl.ds(EXTRA, HEAD)], target.at[own_rows(base), LAST],
            send_last.at[t], recv_last.at[t, j], first + GROUP - 1,
        )

    def load(t):
        return pltpu.make_async_copy(
            tensors[t][0].at[:, head_columns(j)], stage.at[t, :, MAIN], load_sem.at[t, 0]
        )

    def load_last(t):
        return pltpu.make_async_copy(
            tensors[t][0].at[:, pl.ds(EXTRA, HEAD)], stage.at[t, :, LAST], load_sem.at[t, 1]
        )

    def store(t):
        return pltpu.make_async_copy(
            stage.at[t], tensors[t][1].at[own_rows(tensors[t][2]), :], store_sem.at[t]
        )

    for t in range(3):
        for o in ORDER:
            piece(t, o).start()

        @pl.when(j != GROUP - 1)
        def _():
            piece_last(t).start()

        load(t).start()
        load_last(t).start()
    for t in range(3):
        load(t).wait()
        load_last(t).wait()
        store(t).start()
    for t in range(3):
        store(t).wait()

    def arrival(t, s):
        source, target, base = tensors[t]
        rows = pl.ds(base + s * ROWS, ROWS)

        @pl.when(j != s)
        def _():
            remote(
                source.at[:, MAIN], target.at[rows, MAIN], send.at[t, 0], recv.at[t, s], me
            ).wait_recv()

            @pl.when(j == GROUP - 1)
            def _():
                remote(
                    source.at[:, pl.ds(EXTRA, HEAD)], target.at[rows, LAST],
                    send_last.at[t], recv_last.at[t, s], me,
                ).wait_recv()

    def halo(t, s):
        target, base = tensors[t][1:]
        size = SPAN + base
        if s < GROUP // 2:
            start, stop = s * ROWS, min((s + 1) * ROWS, base)
            device, origin, landing = below, base + start, size + start
        else:
            start, stop = max(s * ROWS, SPAN - base), (s + 1) * ROWS
            device, origin, landing = above, base + start, start - (SPAN - base)
        if stop <= start:
            return None
        length = stop - start

        def copy(columns, sends, recvs):
            return remote(
                target.at[pl.ds(origin, length), columns],
                target.at[pl.ds(landing, length), columns],
                sends.at[t, s], recvs.at[t, s], device,
            )

        return copy(MAIN, halo_send, halo_recv), copy(LAST, halo_send_last, halo_recv_last)

    copies = []
    for t in range(3):
        for s in (3, 4, 2, 5, 1, 6, 0, 7):
            arrival(t, s)
            both = halo(t, s)
            if both is not None:
                main, last = both
                main.start()

                @pl.when(j == GROUP - 1)
                def _():
                    last.start()

                copies.append(both)
    for main, last in copies:
        main.wait()

        @pl.when(j == GROUP - 1)
        def _():
            last.wait()

    for t in range(3):
        for o in ORDER:
            piece(t, o).wait_send()

        @pl.when(j != GROUP - 1)
        def _():
            piece_last(t).wait_send()


def spread(keys, values, queries, count):
    shape = jax.ShapeDtypeStruct
    dma = pltpu.SemaphoreType.DMA
    anywhere = pl.BlockSpec(memory_space=pl.ANY)
    return pl.pallas_call(
        functools.partial(spread_kernel, count),
        out_shape=(
            shape((KROWS, FULL), jnp.bfloat16),
            shape((KROWS, FULL), jnp.bfloat16),
            shape((QROWS, FULL), jnp.bfloat16),
        ),
        in_specs=[anywhere] * 3,
        out_specs=(anywhere,) * 3,
        scratch_shapes=[
            pltpu.VMEM((3, ROWS, FULL), jnp.bfloat16),
            dma((3, GROUP)), dma((3, GROUP)), dma((3,)), dma((3, GROUP)),
            dma((3, 2)), dma((3,)),
            dma((3, GROUP)), dma((3, GROUP)), dma((3, GROUP)), dma((3, GROUP)),
        ],
        compiler_params=pltpu.CompilerParams(collective_id=0, has_side_effects=True),
        name="spread",
    )(keys, values, queries)


def collect_kernel(o_in, a_out, stage, send, recv, send_last, recv_last, load_sem, store_sem):
    me = lax.axis_index("seq")
    j = lax.rem(me, GROUP)
    first = me - j
    greet([first + lax.rem(j + o, GROUP) for o in ORDER])

    def rows_of(index):
        return pl.ds(pl.multiple_of(index * ROWS, ROWS), ROWS)

    def piece(o):
        to = lax.rem(j + o, GROUP)
        return remote(
            o_in.at[rows_of(to), MAIN], a_out.at[:, head_columns(j)],
            send.at[o], recv.at[j], first + to,
        )

    def piece_last(o):
        to = lax.rem(j + o, GROUP)
        return remote(
            o_in.at[rows_of(to), LAST], a_out.at[:, pl.ds(EXTRA, HEAD)],
            send_last.at[o], recv_last, first + to,
        )

    load = pltpu.make_async_copy(o_in.at[rows_of(j), :], stage, load_sem)
    store = pltpu.make_async_copy(stage.at[:, MAIN], a_out.at[:, head_columns(j)], store_sem.at[0])
    store_last = pltpu.make_async_copy(
        stage.at[:, LAST], a_out.at[:, pl.ds(EXTRA, HEAD)], store_sem.at[1]
    )
    holder = j == GROUP - 1
    for o in ORDER:
        piece(o).start()

    @pl.when(holder)
    def _():
        for o in ORDER:
            piece_last(o).start()

    load.start()
    load.wait()
    store.start()

    @pl.when(holder)
    def _():
        store_last.start()
        store_last.wait()

    store.wait()
    for s in range(GROUP):

        @pl.when(j != s)
        def _():
            remote(
                o_in.at[pl.ds(0, ROWS), MAIN], a_out.at[:, pl.ds(s * WIDE, WIDE)],
                send.at[0], recv.at[s], me,
            ).wait_recv()

    @pl.when(jnp.logical_not(holder))
    def _():
        remote(
            o_in.at[pl.ds(0, ROWS), LAST], a_out.at[:, pl.ds(EXTRA, HEAD)],
            send_last.at[0], recv_last, me,
        ).wait_recv()

    for o in ORDER:
        piece(o).wait_send()

    @pl.when(holder)
    def _():
        for o in ORDER:
            piece_last(o).wait_send()


def collect(outputs, width):
    dma = pltpu.SemaphoreType.DMA
    anywhere = pl.BlockSpec(memory_space=pl.ANY)
    return pl.pallas_call(
        collect_kernel,
        out_shape=jax.ShapeDtypeStruct((ROWS, width), jnp.bfloat16),
        in_specs=[anywhere],
        out_specs=anywhere,
        scratch_shapes=[
            pltpu.VMEM((ROWS, FULL), jnp.bfloat16),
            dma((GROUP,)), dma((GROUP,)), dma((GROUP,)), dma(()), dma(()), dma((2,)),
        ],
        compiler_params=pltpu.CompilerParams(collective_id=1, has_side_effects=True),
        name="collect",
    )(outputs)


def attend_kernel(
    bounds, where, slots, k_ref, v_ref, q_ref, o_ref,
    query, scores, tops, sums, result,
):
    block = pl.program_id(0)
    merged = ROWS // 4
    row_index = where[0]
    targets = (
        row_index * (SPAN // 4) + block * merged
        + lax.broadcasted_iota(jnp.int32, (merged, 1), 0)
    )
    ends = slots[0:1, :]
    packed = slots[1:2, :]
    past = ends <= 4 * targets
    begin = jnp.max(jnp.where(past, ends, 0), axis=1, keepdims=True)
    found = jnp.min(jnp.where(past, 1 << 30, packed), axis=1, keepdims=True)
    finish = found // 64
    across = 32 - (found - finish * 64)
    half = across // 2
    within = targets - begin // 4
    grid_row = within // half
    grid_col = within - grid_row * half
    source = begin + 2 * grid_row * across + 2 * grid_col
    local = source - (row_index * SPAN - WMAX + block * ROWS)
    picks = jnp.concatenate([local, local + 1, local + across, local + across + 1], axis=0)
    lanes = lax.broadcasted_iota(jnp.int32, (ROWS, QUERY_WINDOW), 1)
    choose = jnp.where(lanes == picks, 1.0, 0.0).astype(jnp.bfloat16)
    window = q_ref[pl.ds(pl.multiple_of(block * ROWS, ROWS), QUERY_WINDOW), :]
    query[...] = jnp.dot(choose, window, preferred_element_type=jnp.float32).astype(jnp.bfloat16)
    offset = row_index * SPAN - MOST
    low_once = begin - offset
    high_once = finish - offset
    low = jnp.concatenate([low_once] * 4, axis=0)
    high = jnp.concatenate([high_once] * 4, axis=0)
    chunk_first = bounds[0, block] // CHUNK
    chunk_stop = (bounds[1, block] + CHUNK - 1) // CHUNK

    def run(heads):
        for h in heads:
            tops[h] = jnp.full((ROWS, HEAD), NEG, jnp.float32)
            sums[h] = jnp.zeros((ROWS, HEAD), jnp.float32)
            result[h] = jnp.zeros((ROWS, HEAD), jnp.float32)

        @pl.loop(chunk_first, chunk_stop)
        def _(c):
            rows = pl.ds(pl.multiple_of(c * CHUNK, CHUNK), CHUNK)
            places = c * CHUNK + lax.broadcasted_iota(jnp.int32, (1, CHUNK), 1)
            kept = (places >= low) & (places < high)
            for h in heads:
                columns = pl.ds(h * HEAD, HEAD)
                part = lax.dot_general(
                    query[:, columns], k_ref[rows, columns], (((1,), (1,)), ((), ())),
                    preferred_element_type=jnp.float32,
                )
                part = jnp.where(kept, part, NEG)
                scores[h, c - chunk_first] = part
                best = tops[h]
                for g in range(CHUNK // HEAD):
                    best = jnp.maximum(best, part[:, g * HEAD:(g + 1) * HEAD])
                tops[h] = best

        for h in heads:
            tops[h] = jnp.broadcast_to(
                jnp.max(tops[h], axis=1, keepdims=True), (ROWS, HEAD)
            )

        @pl.loop(chunk_first, chunk_stop)
        def _(c):
            rows = pl.ds(pl.multiple_of(c * CHUNK, CHUNK), CHUNK)
            for h in heads:
                columns = pl.ds(h * HEAD, HEAD)
                top = jnp.concatenate([tops[h]] * (CHUNK // HEAD), axis=1)
                weights = jnp.exp2((scores[h, c - chunk_first] - top) * EXP_SCALE)
                total = sums[h]
                for g in range(CHUNK // HEAD):
                    total = total + weights[:, g * HEAD:(g + 1) * HEAD]
                sums[h] = total
                result[h] += jnp.dot(
                    weights.astype(jnp.bfloat16), v_ref[rows, columns],
                    preferred_element_type=jnp.float32,
                )

        for h in heads:
            total = jnp.sum(sums[h], axis=1, keepdims=True)
            o_ref[:, pl.ds(h * HEAD, HEAD)] = (result[h] / total).astype(jnp.bfloat16)

    @pl.when(where[1] == GROUP - 1)
    def _():
        run((0, 1, 2, 3))

    @pl.when(where[1] != GROUP - 1)
    def _():
        run((0, 1, 2))


def attend(bounds, where, slots, keys, values, queries):
    whole = lambda shape: pl.BlockSpec(shape, lambda i, *_: (0, 0), pipeline_mode=pl.Buffered(1))
    return pl.pallas_call(
        attend_kernel,
        out_shape=jax.ShapeDtypeStruct((SPAN, FULL), jnp.bfloat16),
        grid_spec=pltpu.PrefetchScalarGridSpec(
            num_scalar_prefetch=2,
            grid=(GROUP,),
            in_specs=[
                whole(slots.shape), whole(keys.shape), whole(values.shape), whole(queries.shape)
            ],
            out_specs=pl.BlockSpec((ROWS, FULL), lambda i, *_: (i, 0)),
            scratch_shapes=[
                pltpu.VMEM((ROWS, FULL), jnp.bfloat16),
                pltpu.VMEM((4, CHUNKS, ROWS, CHUNK), jnp.float32),
                pltpu.VMEM((4, ROWS, HEAD), jnp.float32),
                pltpu.VMEM((4, ROWS, HEAD), jnp.float32),
                pltpu.VMEM((4, ROWS, HEAD), jnp.float32),
            ],
        ),
        name="attend",
    )(bounds, where, slots, keys, values, queries)


def norm_kernel(width, a_ref, gain_ref, bias_ref, o_ref):
    parts = [a_ref[g].astype(jnp.float32) for g in range(4)]
    features = 4 * width
    center = sum(jnp.sum(p, axis=1, keepdims=True) for p in parts) / features
    spread_sum = sum(jnp.sum(jnp.square(p - center), axis=1, keepdims=True) for p in parts)
    scale = lax.rsqrt(spread_sum / features + 1e-06)
    for g in range(4):
        columns = pl.ds(g * width, width)
        o_ref[:, columns] = (
            (parts[g] - center) * scale * gain_ref[:, columns] + bias_ref[:, columns]
        ).astype(jnp.bfloat16)


def norm(attention, gain, bias):
    rows, width = attention.shape
    merged = rows // 4
    step = 16
    fixed = pl.BlockSpec((1, 4 * width), lambda i: (0, 0))
    return pl.pallas_call(
        functools.partial(norm_kernel, width),
        out_shape=jax.ShapeDtypeStruct((merged, 4 * width), jnp.bfloat16),
        grid=(merged // step,),
        in_specs=[pl.BlockSpec((4, step, width), lambda i: (0, i, 0)), fixed, fixed],
        out_specs=pl.BlockSpec((step, 4 * width), lambda i: (i, 0)),
        name="norm",
    )(attention.reshape(4, merged, width), gain.reshape(1, -1), bias.reshape(1, -1))


def body(queries, keys, values, img_height, img_width, norm_gain, norm_bias):
    count = lax.axis_size("seq")
    device = lax.axis_index("seq")
    row_index = device // GROUP
    ends = jnp.cumsum(img_height * img_width)
    packed = ends * 64 + (32 - img_width)
    slot_count = ends.shape[0]
    pad = -slot_count % 128
    last = jnp.full((pad,), 1 << 30, jnp.int32)
    slots = jnp.stack([jnp.concatenate([ends, last]), jnp.concatenate([packed, last])])
    firsts = 4 * (row_index * (SPAN // 4) + jnp.arange(GROUP, dtype=jnp.int32) * (ROWS // 4))
    lows = jnp.max(jnp.where(ends[None, :] <= firsts[:, None], ends[None, :], 0), axis=1)
    finals = firsts + ROWS - 4
    highs = jnp.min(jnp.where(ends[None, :] > finals[:, None], ends[None, :], 1 << 30), axis=1)
    bounds = jnp.stack([lows, highs]) - (row_index * SPAN - MOST)
    where = jnp.stack([row_index, device % GROUP])
    k_row, v_row, q_row = spread(keys, values, queries, count)
    outputs = attend(bounds, where, slots, k_row, v_row, q_row)
    return norm(collect(outputs, queries.shape[1]), norm_gain, norm_bias)


def solution(mesh):
    in_specs = (P("seq", None), P("seq", None), P("seq", None), P(), P(), P(), P())
    out_specs = P("seq", None)
    return jax.shard_map(body, mesh=mesh, in_specs=in_specs, out_specs=out_specs, check_vma=False)
```

time: 580 us -> 151 us (0.26)
  waiting for transfers between devices: 253 us -> 0 us
  local copies, waits for them, and re-layouts: 165 us -> 1.52 us
  Pallas kernels: 0 us -> 144 us
  matrix products: 84.2 us -> 0 us
  starting transfers between devices: 54.3 us -> 0 us
  other arithmetic: 18.9 us -> 4.48 us
    ppermute x18 -> x0, waiting for transfers between devices: 253 us -> none  [the longest x16 249 us: shifted(): return lax.ppermute(block, axis, route)]
    gather x26 -> x0, local copies, waits for them, and re-layouts: 148 us -> none  [the longest x22 144 us: image_index(): return jnp.searchsorted(image_ends, positions, side='right')]
    pallas_call x0 -> x4, Pallas kernels: none -> 144 us  [the longest x1 64.2 us: spread(): pl.pallas_call(functools.partial(spread_kernel, count), out_shape=(shape(...]
    dot_general x50 -> x0, matrix products: 84.2 us -> none  [the longest x25 42.3 us: one_head(): lax.dot_general(q_head, k_head, (((1,), (1,)), ((), ())), preferred_eleme...]
    ppermute x18 -> x0, starting transfers between devices: 54.3 us -> none  [the longest x16 46 us: shifted(): return lax.ppermute(block, axis, route)]
    unnamed x36 -> x5, local copies, waits for them, and re-layouts: 15.8 us -> 0.01 us
    reduce_sum x28 -> x0, other arithmetic: 15.1 us -> none  [the longest x25 11.9 us: one_head(): totals = jnp.sum(weights, axis=1, keepdims=True)]
  transfers between devices with their start and end apart: 18 -> 0, of which waited for: 10 -> 0; matrix products, arithmetic and copies ran while one was open for 27% -> 0% of each run, Pallas kernels for 0% -> 0%
where the time goes in v1:
time: 151 us; the launch traced here: 150 us
  Pallas kernels  144 us (95%)
  other arithmetic  4.48 us (3%)
  local copies, waits for them, and re-layouts  1.52 us (1%)
    pallas_call x1, Pallas kernels, spread(): pl.pallas_call(functools.partial(spread_kernel, count), out_shape=(shape(...  64.2 us
    pallas_call x1, Pallas kernels, attend(): pl.pallas_call(attend_kernel, out_shape=jax.ShapeDtypeStruct((SPAN, FULL)...  40.3 us
    pallas_call x1, Pallas kernels, collect(): pl.pallas_call(collect_kernel, out_shape=jax.ShapeDtypeStruct((ROWS, widt...  35 us
    pallas_call x1, Pallas kernels, norm(): pl.pallas_call(functools.partial(norm_kernel, width), out_shape=jax.Shape...  4.49 us

profile of v1, /device:TPU:5, one launch (start us, length us, event | category | flops | bytes accessed | tf_op | source)
XLA Modules:
  0.0 150.0 jit_solution(3065067230564728748)
XLA Ops:
  0.0 0.6 pad_add_fusion.1.where
  0.6 0.7 mul.35
  1.3 0.3 reduce-window.9
  1.6 0.1 slice.14
  1.7 0.1 slice_reduce_fusion
  1.8 0.8 select_bitcast_fusion
  2.6 0.7 subtract_add_fusion
  3.3 0.2 select_reduce_fusion.1
  3.5 0.5 add_subtract_fusion.bounds
  4.1 0.6 pad_add_fusion.slots
  4.7 64.2 %spread.1 = (bf16[3840,512]{1,0:T(8,128)(2,1)}, bf16[3840,512]{1,0:T(8,128)(2,1)}, bf16[2112,512]{1,0:T(8,128)(2,1)}) custom-call(bf16[256,3200]{1,0:T(8,128)(2,1)} %k_in.1, bf16[256,3200]{1,0:T(8,128)(2,1)} %v_in.1, bf16[256,3200]{1,0:T(8,128)(2,1)} %q_in.1), custom_call_target="tpu_custom_call" | custom-call | tf_op jit(solution)/shard_map/spread/pallas_call | solution.py:194
  68.9 40.3 %attend.1.o_in = bf16[2048,512]{1,0:T(8,128)(2,1)} custom-call(s32[2,8]{1,0:T(2,128)} %add_subtract_fusion.bounds, s32[2]{0:T(128)} %pad_add_fusion.1.where, s32[2,1152]{1,0:T(2,128)} %pad_add_fusion.slots, bf16[3840,512]{1,0:T(8,128)(2,1)} %get-tuple-element.8.k_ref, bf16[3840,512]{1,0:T(8,128)(2,1)} %get-tuple-element.9.v_ref, ...), custom_call_target="tpu_custom_call" | custom-call | tf_op jit(solution)/shard_map/attend/pallas_call | solution.py:400
  109.2 0.0 copy-start
  109.2 0.0 copy-start.1
  109.2 35.0 %collect.1 = bf16[256,3200]{1,0:T(8,128)(2,1)} custom-call(bf16[2048,512]{1,0:T(8,128)(2,1)} %attend.1.o_in), custom_call_target="tpu_custom_call" | custom-call | tf_op jit(solution)/shard_map/collect/pallas_call | solution.py:289
  144.2 0.0 copy-done
  144.2 0.7 reshape.54.gain_ref
  144.8 0.0 copy-done.1
  144.8 0.6 reshape.55.bias_ref
  145.5 4.5 %norm.1 = bf16[64,12800]{1,0:T(8,128)(2,1)} custom-call(bf16[4,64,3200]{2,1,0:T(8,128)(2,1)} %bitcast.15, f32[1,12800]{1,0:T(1,128)} %reshape.54.gain_ref, f32[1,12800]{1,0:T(1,128)} %reshape.55.bias_ref), custom_call_target="tpu_custom_call" | custom-call | tf_op jit(solution)/shard_map/norm/pallas_call | solution.py:440
  (6 shorter events, 0.1 us)
Async XLA Ops:
  109.2 35.0 %copy-start = (f32[12800]{0:T(1024)S(1)}, f32[12800]{0:T(1024)}, u32[]{:S(2)}) copy-start(f32[12800]{0:T(1024)} %param.12) | copy-start | bytes 153604
  109.2 35.6 %copy-start.1 = (f32[12800]{0:T(1024)S(1)}, f32[12800]{0:T(1024)}, u32[]{:S(2)}) copy-start(f32[12800]{0:T(1024)} %param.13) | copy-start | bytes 153604

commit v2 on v0

v2 whole, which is shorter than its diff:
```python
import functools
import math

import jax
import jax.numpy as jnp
from jax import lax
from jax.experimental import pallas as pl
from jax.experimental.pallas import tpu as pltpu
from jax.sharding import PartitionSpec as P

HEAD = 128
MOST = 896
WMAX = 32
GROUP = 8
ROWS = 256
HEADS = 3
ALL_HEADS = GROUP * HEADS + 1
MERGED = ROWS // 4
SPAN = GROUP * ROWS
KROWS = SPAN + 2 * MOST
QROWS = SPAN + 2 * WMAX
WINDOW = 2048
CHUNK = 512
QUERY_WINDOW = ROWS + 2 * WMAX
MESH = pl.DeviceIdType.MESH
NEG = -1e30
EXP_SCALE = math.log2(math.e) / math.sqrt(HEAD)
ORDER = (4, 3, 5, 2, 6, 1, 7)
SOURCES = (3, 4, 2, 5, 1, 6, 0, 7)


def remote(src, dst, send, recv, device):
    return pltpu.make_async_remote_copy(
        src_ref=src,
        dst_ref=dst,
        send_sem=send,
        recv_sem=recv,
        device_id=(device,),
        device_id_type=MESH,
    )


def greet(devices):
    barrier = pltpu.get_barrier_semaphore()
    for device in devices:
        pl.semaphore_signal(barrier, inc=1, device_id=(device,), device_id_type=MESH)
    pl.semaphore_wait(barrier, len(devices))


def spread_lanes(column):
    return jnp.broadcast_to(column, (column.shape[0], HEAD))


def four(column):
    return jnp.concatenate([column] * 4, axis=0)


def plan_blocks(row_index, slots, picks_ref, mask_ref):
    slot_rows = slots.shape[1]

    @pl.loop(0, GROUP)
    def _(i):
        targets = (
            row_index * (SPAN // 4) + i * MERGED
            + lax.broadcasted_iota(jnp.int32, (MERGED, HEAD), 0)
        )
        begin = jnp.zeros((MERGED, HEAD), jnp.int32)
        found = jnp.full((MERGED, HEAD), 1 << 30, jnp.int32)
        for r in range(slot_rows):
            ends = slots[0, r:r + 1, :]
            past = ends <= 4 * targets
            begin = jnp.maximum(begin, jnp.where(past, ends, 0))
            found = jnp.minimum(found, jnp.where(past, 1 << 30, slots[1, r:r + 1, :]))
        begin = spread_lanes(jnp.max(begin, axis=1, keepdims=True))
        found = spread_lanes(jnp.min(found, axis=1, keepdims=True))
        finish = lax.shift_right_logical(found, 6)
        across = 32 - (found & 63)
        half = lax.shift_right_logical(across, 1)
        within = targets - lax.shift_right_logical(begin, 2)
        grid_row = (
            (within.astype(jnp.float32) + 0.5) / half.astype(jnp.float32)
        ).astype(jnp.int32)
        grid_col = within - grid_row * half
        source = begin + 2 * grid_row * across + 2 * grid_col
        local = source - (row_index * SPAN - WMAX + i * ROWS)
        rows = pl.ds(pl.multiple_of(i * ROWS, ROWS), ROWS)
        picks_ref[rows, :] = jnp.concatenate(
            [local, local + 1, local + across, local + across + 1], axis=0
        )
        offset = row_index * SPAN - MOST + i * ROWS
        low, high = begin - offset, finish - offset
        lane = lax.broadcasted_iota(jnp.int32, (MERGED, HEAD), 1)
        for g in range(WINDOW // HEAD):
            place = lane + g * HEAD
            kept = jnp.where((place >= low) & (place < high), 0.0, NEG)
            mask_ref[rows, pl.ds(g * HEAD, HEAD)] = four(kept)


def attend_block(i, q_buf, k_buf, v_buf, picks_ref, mask_ref, scores):
    base = pl.multiple_of(i * ROWS, ROWS)
    rows = pl.ds(base, ROWS)
    picks = picks_ref[rows, :]
    lane = lax.broadcasted_iota(jnp.int32, (ROWS, HEAD), 1)
    choose = jnp.concatenate(
        [jnp.where(lane + g * HEAD == picks, 1.0, 0.0) for g in range(3)], axis=1
    )[:, :QUERY_WINDOW].astype(jnp.bfloat16)
    query = jnp.dot(
        choose, q_buf[pl.ds(base, QUERY_WINDOW), :], preferred_element_type=jnp.float32
    ).astype(jnp.bfloat16)
    best = jnp.full((ROWS, HEAD), NEG, jnp.float32)
    for c in range(WINDOW // CHUNK):
        part = lax.dot_general(
            query, k_buf[pl.ds(base + c * CHUNK, CHUNK), :], (((1,), (1,)), ((), ())),
            preferred_element_type=jnp.float32,
        ) + mask_ref[rows, pl.ds(c * CHUNK, CHUNK)]
        scores[:, pl.ds(c * CHUNK, CHUNK)] = part
        for g in range(CHUNK // HEAD):
            best = jnp.maximum(best, part[:, g * HEAD:(g + 1) * HEAD])
    top = spread_lanes(jnp.max(best, axis=1, keepdims=True))
    tops = jnp.concatenate([top] * (CHUNK // HEAD), axis=1)
    total = jnp.zeros((ROWS, HEAD), jnp.float32)
    result = jnp.zeros((ROWS, HEAD), jnp.float32)
    for c in range(WINDOW // CHUNK):
        weights = jnp.exp2((scores[:, pl.ds(c * CHUNK, CHUNK)] - tops) * EXP_SCALE)
        for g in range(CHUNK // HEAD):
            total = total + weights[:, g * HEAD:(g + 1) * HEAD]
        result = result + jnp.dot(
            weights.astype(jnp.bfloat16), v_buf[pl.ds(base + c * CHUNK, CHUNK), :],
            preferred_element_type=jnp.float32,
        )
    return (result / jnp.sum(total, axis=1, keepdims=True)).astype(jnp.bfloat16)


def normalize(landed, gain_ref, bias_ref, out_ref):
    step = 16
    features = 4 * ALL_HEADS * HEAD

    @pl.loop(0, MERGED // step)
    def _(g):
        first = pl.multiple_of(g * step, step)

        def tile(quarter, head):
            start = pl.multiple_of(quarter * MERGED + first, step)
            return landed[head, pl.ds(start, step), :].astype(jnp.float32)

        places = [(q, h) for q in range(4) for h in range(ALL_HEADS)]
        total = sum(tile(*place) for place in places)
        center = spread_lanes(jnp.sum(total, axis=1, keepdims=True) / features)
        squares = sum(jnp.square(tile(*place) - center) for place in places)
        scale = spread_lanes(
            lax.rsqrt(jnp.sum(squares, axis=1, keepdims=True) / features + 1e-06)
        )
        for index, place in enumerate(places):
            out_ref[pl.ds(first, step), pl.ds(index * HEAD, HEAD)] = (
                (tile(*place) - center) * scale * gain_ref[index:index + 1, :]
                + bias_ref[index:index + 1, :]
            ).astype(jnp.bfloat16)


def kernel(
    count, slots, k_in, v_in, q_in, gain_ref, bias_ref, out_ref,
    k_buf, v_buf, q_buf, outs, landed, picks_ref, mask_ref, scores,
    send, recv, load_sem, halo_send, halo_recv, out_send, out_recv,
):
    me = lax.axis_index("seq")
    j = lax.rem(me, GROUP)
    first = me - j
    row_index = me // GROUP
    above = lax.rem(me + GROUP, count)
    below = lax.rem(me + count - GROUP, count)
    holder = j == GROUP - 1
    greet([first + lax.rem(j + o, GROUP) for o in ORDER] + [above, below])
    tensors = ((k_in, k_buf, MOST), (v_in, v_buf, MOST), (q_in, q_buf, WMAX))

    def columns_of(index, n):
        head = GROUP * HEADS if n == HEADS else index * HEADS + n
        return pl.ds(pl.multiple_of(head * HEAD, HEAD), HEAD)

    def own_rows(base):
        return pl.ds(pl.multiple_of(base + j * ROWS, 32), ROWS)

    def piece(n, t, o):
        source, target, base = tensors[t]
        to = GROUP - 1 if n == HEADS else lax.rem(j + o, GROUP)
        return remote(
            source.at[:, columns_of(to, n)], target.at[n, own_rows(base), :],
            send.at[n, t, o], recv.at[n, t, j], first + to,
        )

    def own(n, t):
        source, target, base = tensors[t]
        return pltpu.make_async_copy(
            source.at[:, columns_of(j, n)], target.at[n, own_rows(base), :], load_sem.at[n, t]
        )

    def each_piece(n, act):
        for t in range(3):
            if n == HEADS:

                @pl.when(jnp.logical_not(holder))
                def _():
                    act(piece(n, t, 0))

            else:
                for o in ORDER:
                    act(piece(n, t, o))

    def start_stage(n):
        each_piece(n, lambda copy: copy.start())
        for t in range(3):
            if n == HEADS:

                @pl.when(holder)
                def _():
                    own(n, t).start()

            else:
                own(n, t).start()

    def halo(n, t, s):
        target, base = tensors[t][1:]
        if s < GROUP // 2:
            start, stop = s * ROWS, min((s + 1) * ROWS, base)
            device, landing = below, base + SPAN + start
        else:
            start, stop = max(s * ROWS, SPAN - base), (s + 1) * ROWS
            device, landing = above, start - (SPAN - base)
        if stop <= start:
            return None
        return remote(
            target.at[n, pl.ds(base + start, stop - start), :],
            target.at[n, pl.ds(landing, stop - start), :],
            halo_send.at[n, t, s], halo_recv.at[n, t, s], device,
        )

    def arrive(n):
        for t in range(3):
            for s in SOURCES:
                source, target, base = tensors[t]

                @pl.when(j != s)
                def _():
                    remote(
                        source.at[:, pl.ds(0, HEAD)],
                        target.at[n, pl.ds(base + s * ROWS, ROWS), :],
                        send.at[n, t, 0], recv.at[n, t, s], me,
                    ).wait_recv()

                @pl.when(j == s)
                def _():
                    own(n, t).wait()

                copy = halo(n, t, s)
                if copy is not None:
                    copy.start()
        for t in range(3):
            for s in SOURCES:
                copy = halo(n, t, s)
                if copy is not None:
                    copy.wait_recv()

    def output(n, i):
        head = GROUP * HEADS if n == HEADS else j * HEADS + n
        rows = pl.ds(pl.multiple_of(i * ROWS, ROWS), ROWS)
        return remote(
            outs.at[n, rows, :], landed.at[head], out_send.at[n, i], out_recv.at[n, j], first + i
        )

    def compute(n):
        head = GROUP * HEADS if n == HEADS else j * HEADS + n

        @pl.loop(0, GROUP)
        def _(i):
            block = attend_block(
                i, q_buf.at[n], k_buf.at[n], v_buf.at[n], picks_ref, mask_ref, scores
            )
            outs[n, pl.ds(pl.multiple_of(i * ROWS, ROWS), ROWS), :] = block

            @pl.when(i == j)
            def _():
                landed[head] = block

            @pl.when((i > 0) & (i - 1 != j))
            def _():
                output(n, i - 1).start()

        @pl.when(jnp.logical_not(holder))
        def _():
            output(n, GROUP - 1).start()

    start_stage(0)
    start_stage(1)
    plan_blocks(row_index, slots, picks_ref, mask_ref)
    arrive(0)
    start_stage(3)
    start_stage(2)
    compute(0)
    arrive(1)
    compute(1)

    @pl.when(holder)
    def _():
        arrive(3)
        compute(3)

    arrive(2)
    compute(2)

    for n in range(HEADS):
        for s in range(GROUP):

            @pl.when(j != s)
            def _():
                remote(
                    outs.at[n, pl.ds(0, ROWS), :], landed.at[s * HEADS + n],
                    out_send.at[n, 0], out_recv.at[n, s], me,
                ).wait_recv()

    @pl.when(jnp.logical_not(holder))
    def _():
        remote(
            outs.at[HEADS, pl.ds(0, ROWS), :], landed.at[GROUP * HEADS],
            out_send.at[HEADS, 0], out_recv.at[HEADS, GROUP - 1], me,
        ).wait_recv()

    normalize(landed, gain_ref, bias_ref, out_ref)

    def finish(n):
        for t in range(3):
            for s in SOURCES:
                copy = halo(n, t, s)
                if copy is not None:
                    copy.wait_send()
        for i in range(GROUP):

            @pl.when(j != i)
            def _():
                output(n, i).wait_send()

    for n in range(HEADS + 1):
        each_piece(n, lambda copy: copy.wait_send())
        if n == HEADS:
            pl.when(holder)(functools.partial(finish, n))
        else:
            finish(n)


def body(queries, keys, values, img_height, img_width, norm_gain, norm_bias):
    count = lax.axis_size("seq")
    features = norm_gain.shape[0]
    ends = jnp.cumsum(img_height * img_width)
    packed = ends * 64 + (32 - img_width)
    pad = -ends.shape[0] % HEAD
    slots = jnp.pad(
        jnp.stack([ends, packed]), ((0, 0), (0, pad)), constant_values=1 << 30
    ).reshape(2, -1, HEAD)
    dma = pltpu.SemaphoreType.DMA
    anywhere = pl.BlockSpec(memory_space=pl.ANY)
    resident = pl.BlockSpec(memory_space=pltpu.VMEM)
    stages = HEADS + 1
    return pl.pallas_call(
        functools.partial(kernel, count),
        out_shape=jax.ShapeDtypeStruct((MERGED, features), jnp.bfloat16),
        in_specs=[resident, anywhere, anywhere, anywhere, resident, resident],
        out_specs=resident,
        scratch_shapes=[
            pltpu.VMEM((stages, KROWS, HEAD), jnp.bfloat16),
            pltpu.VMEM((stages, KROWS, HEAD), jnp.bfloat16),
            pltpu.VMEM((stages, QROWS, HEAD), jnp.bfloat16),
            pltpu.VMEM((stages, SPAN, HEAD), jnp.bfloat16),
            pltpu.VMEM((ALL_HEADS, ROWS, HEAD), jnp.bfloat16),
            pltpu.VMEM((SPAN, HEAD), jnp.int32),
            pltpu.VMEM((SPAN, WINDOW), jnp.float32),
            pltpu.VMEM((ROWS, WINDOW), jnp.float32),
            dma((stages, 3, GROUP)), dma((stages, 3, GROUP)), dma((stages, 3)),
            dma((stages, 3, GROUP)), dma((stages, 3, GROUP)),
            dma((stages, GROUP)), dma((stages, GROUP)),
        ],
        compiler_params=pltpu.CompilerParams(
            collective_id=0, has_side_effects=True, vmem_limit_bytes=60 * 1024 * 1024
        ),
        name="packed_attention",
    )(
        slots, keys, values, queries,
        norm_gain.reshape(-1, HEAD), norm_bias.reshape(-1, HEAD),
    )


def solution(mesh):
    in_specs = (P("seq", None), P("seq", None), P("seq", None), P(), P(), P(), P())
    out_specs = P("seq", None)
    return jax.shard_map(body, mesh=mesh, in_specs=in_specs, out_specs=out_specs, check_vma=False)
```

time: 580 us -> 120 us (0.21)
  waiting for transfers between devices: 253 us -> 0 us
  local copies, waits for them, and re-layouts: 165 us -> 3.53 us
  Pallas kernels: 0 us -> 114 us
  matrix products: 84.2 us -> 0 us
  starting transfers between devices: 54.3 us -> 0 us
  other arithmetic: 18.9 us -> 1.82 us
    ppermute x18 -> x0, waiting for transfers between devices: 253 us -> none  [the longest x16 249 us: shifted(): return lax.ppermute(block, axis, route)]
    gather x26 -> x0, local copies, waits for them, and re-layouts: 148 us -> none  [the longest x22 144 us: image_index(): return jnp.searchsorted(image_ends, positions, side='right')]
    pallas_call x0 -> x1, Pallas kernels: none -> 114 us  [body(): pl.pallas_call(functools.partial(kernel, count), out_shape=jax.ShapeDtype...]
    dot_general x50 -> x0, matrix products: 84.2 us -> none  [the longest x25 42.3 us: one_head(): lax.dot_general(q_head, k_head, (((1,), (1,)), ((), ())), preferred_eleme...]
    ppermute x18 -> x0, starting transfers between devices: 54.3 us -> none  [the longest x16 46 us: shifted(): return lax.ppermute(block, axis, route)]
    reduce_sum x28 -> x0, other arithmetic: 15.1 us -> none  [the longest x25 11.9 us: one_head(): totals = jnp.sum(weights, axis=1, keepdims=True)]
    unnamed x36 -> x1, local copies, waits for them, and re-layouts: 15.8 us -> 2.7 us
  transfers between devices with their start and end apart: 18 -> 0, of which waited for: 10 -> 0; matrix products, arithmetic and copies ran while one was open for 27% -> 0% of each run, Pallas kernels for 0% -> 0%
where the time goes in v2:
time: 120 us
  Pallas kernels  114 us (95%)
  local copies, waits for them, and re-layouts  3.53 us (3%)
  other arithmetic  1.82 us (2%)
    pallas_call x1, Pallas kernels, body(): pl.pallas_call(functools.partial(kernel, count), out_shape=jax.ShapeDtype...  114 us
    unnamed x1, local copies, waits for them, and re-layouts  2.7 us

profile of v2, /device:TPU:5, one launch (start us, length us, event | category | flops | bytes accessed | tf_op | source)
XLA Modules:
  0.0 119.7 jit_solution(3105594958806577130)
XLA Ops:
  0.0 0.7 mul.9
  0.7 0.3 reduce-window.9
  1.0 0.1 slice.13
  1.1 0.1 slice_reduce_fusion
  1.2 0.1 add_bitcast_fusion
  1.3 0.7 fusion
  2.1 0.6 reshape.25.slots
  2.7 114.3 %packed_attention.1 = bf16[64,12800]{1,0:T(8,128)(2,1)} custom-call(s32[2,9,128]{2,1,0:T(8,128)} %reshape.25.slots, bf16[256,3200]{1,0:T(8,128)(2,1)} %k_in.1, bf16[256,3200]{1,0:T(8,128)(2,1)} %v_in.1, bf16[256,3200]{1,0:T(8,128)(2,1)} %q_in.1, f32[100,128]{1,0:T(8,128)} %bitcast.6, f32[100,128]{1,0:T(8,128)} %bitcast.7), custom_call_target="tpu_custom_call" | custom-call | tf_op jit(solution)/shard_map/packed_attention/pallas_call | solution.py:361
  117.0 2.7 %copy.9 = bf16[64,12800]{1,0:T(8,128)(2,1)} copy(bf16[64,12800]{1,0:T(8,128)(2,1)} %packed_attention.1) | data formatting | bytes 3276800
  (6 shorter events, 0.1 us)

commit v3 on v2

--- a/solution.py
+++ b/solution.py
@@ -96,38 +96,62 @@
             mask_ref[rows, pl.ds(g * HEAD, HEAD)] = four(kept)
 
 
-def attend_block(i, q_buf, k_buf, v_buf, picks_ref, mask_ref, scores):
+def pick_queries(i, q_buf, picks_ref):
     base = pl.multiple_of(i * ROWS, ROWS)
-    rows = pl.ds(base, ROWS)
-    picks = picks_ref[rows, :]
+    picks = picks_ref[pl.ds(base, ROWS), :]
     lane = lax.broadcasted_iota(jnp.int32, (ROWS, HEAD), 1)
     choose = jnp.concatenate(
         [jnp.where(lane + g * HEAD == picks, 1.0, 0.0) for g in range(3)], axis=1
     )[:, :QUERY_WINDOW].astype(jnp.bfloat16)
-    query = jnp.dot(
+    return jnp.dot(
         choose, q_buf[pl.ds(base, QUERY_WINDOW), :], preferred_element_type=jnp.float32
     ).astype(jnp.bfloat16)
-    best = jnp.full((ROWS, HEAD), NEG, jnp.float32)
+
+
+def score_chunk(query, i, c, best, k_buf, mask_ref, scores):
+    base = pl.multiple_of(i * ROWS, ROWS)
+    part = lax.dot_general(
+        query, k_buf[pl.ds(base + c * CHUNK, CHUNK), :], (((1,), (1,)), ((), ())),
+        preferred_element_type=jnp.float32,
+    ) + mask_ref[pl.ds(base, ROWS), pl.ds(c * CHUNK, CHUNK)]
+    scores[:, pl.ds(c * CHUNK, CHUNK)] = part
+    for g in range(CHUNK // HEAD):
+        best = jnp.maximum(best, part[:, g * HEAD:(g + 1) * HEAD])
+    return best
+
+
+def lowest():
+    return jnp.full((ROWS, HEAD), NEG, jnp.float32)
+
+
+def first_scores(q_buf, k_buf, picks_ref, mask_ref, scores, tops):
+    query = pick_queries(0, q_buf, picks_ref)
+    best = lowest()
     for c in range(WINDOW // CHUNK):
-        part = lax.dot_general(
-            query, k_buf[pl.ds(base + c * CHUNK, CHUNK), :], (((1,), (1,)), ((), ())),
-            preferred_element_type=jnp.float32,
-        ) + mask_ref[rows, pl.ds(c * CHUNK, CHUNK)]
-        scores[:, pl.ds(c * CHUNK, CHUNK)] = part
-        for g in range(CHUNK // HEAD):
-            best = jnp.maximum(best, part[:, g * HEAD:(g + 1) * HEAD])
-    top = spread_lanes(jnp.max(best, axis=1, keepdims=True))
-    tops = jnp.concatenate([top] * (CHUNK // HEAD), axis=1)
+        best = score_chunk(query, 0, c, best, k_buf, mask_ref, scores)
+    tops[...] = spread_lanes(jnp.max(best, axis=1, keepdims=True))
+
+
+def attend_step(i, q_buf, k_buf, v_buf, picks_ref, mask_ref, now, later):
+    scores, tops = now
+    later_scores, later_tops = later
+    base = pl.multiple_of(i * ROWS, ROWS)
+    following = jnp.minimum(i + 1, GROUP - 1)
+    query = pick_queries(following, q_buf, picks_ref)
+    best = lowest()
+    top = jnp.concatenate([tops[...]] * (CHUNK // HEAD), axis=1)
     total = jnp.zeros((ROWS, HEAD), jnp.float32)
     result = jnp.zeros((ROWS, HEAD), jnp.float32)
     for c in range(WINDOW // CHUNK):
-        weights = jnp.exp2((scores[:, pl.ds(c * CHUNK, CHUNK)] - tops) * EXP_SCALE)
+        best = score_chunk(query, following, c, best, k_buf, mask_ref, later_scores)
+        weights = jnp.exp2((scores[:, pl.ds(c * CHUNK, CHUNK)] - top) * EXP_SCALE)
         for g in range(CHUNK // HEAD):
             total = total + weights[:, g * HEAD:(g + 1) * HEAD]
         result = result + jnp.dot(
             weights.astype(jnp.bfloat16), v_buf[pl.ds(base + c * CHUNK, CHUNK), :],
             preferred_element_type=jnp.float32,
         )
+    later_tops[...] = spread_lanes(jnp.max(best, axis=1, keepdims=True))
     return (result / jnp.sum(total, axis=1, keepdims=True)).astype(jnp.bfloat16)
 
 
@@ -159,7 +183,8 @@
 
 def kernel(
     count, slots, k_in, v_in, q_in, gain_ref, bias_ref, out_ref,
-    k_buf, v_buf, q_buf, outs, landed, picks_ref, mask_ref, scores,
+    k_buf, v_buf, q_buf, outs, landed, picks_ref, mask_ref,
+    scores_a, scores_b, tops_a, tops_b,
     send, recv, load_sem, halo_send, halo_recv, out_send, out_recv,
 ):
     me = lax.axis_index("seq")
@@ -193,8 +218,8 @@
             source.at[:, columns_of(j, n)], target.at[n, own_rows(base), :], load_sem.at[n, t]
         )
 
-    def each_piece(n, act):
-        for t in range(3):
+    def each_piece(n, act, only=(0, 1, 2)):
+        for t in only:
             if n == HEADS:
 
                 @pl.when(jnp.logical_not(holder))
@@ -205,9 +230,9 @@
                 for o in ORDER:
                     act(piece(n, t, o))
 
-    def start_stage(n):
-        each_piece(n, lambda copy: copy.start())
-        for t in range(3):
+    def depart(n, only=(0, 1, 2)):
+        each_piece(n, lambda copy: copy.start(), only)
+        for t in only:
             if n == HEADS:
 
                 @pl.when(holder)
@@ -233,8 +258,8 @@
             halo_send.at[n, t, s], halo_recv.at[n, t, s], device,
         )
 
-    def arrive(n):
-        for t in range(3):
+    def arrive(n, only=(0, 1, 2)):
+        for t in only:
             for s in SOURCES:
                 source, target, base = tensors[t]
 
@@ -253,6 +278,8 @@
                 copy = halo(n, t, s)
                 if copy is not None:
                     copy.start()
+
+    def complete(n):
         for t in range(3):
             for s in SOURCES:
                 copy = halo(n, t, s)
@@ -266,13 +293,14 @@
             outs.at[n, rows, :], landed.at[head], out_send.at[n, i], out_recv.at[n, j], first + i
         )
 
-    def compute(n):
+    def compute(n, events=()):
         head = GROUP * HEADS if n == HEADS else j * HEADS + n
 
-        @pl.loop(0, GROUP)
-        def _(i):
-            block = attend_block(
-                i, q_buf.at[n], k_buf.at[n], v_buf.at[n], picks_ref, mask_ref, scores
+        first_scores(q_buf.at[n], k_buf.at[n], picks_ref, mask_ref, scores_a, tops_a)
+
+        def block_step(i, now, later):
+            block = attend_step(
+                i, q_buf.at[n], k_buf.at[n], v_buf.at[n], picks_ref, mask_ref, now, later
             )
             outs[n, pl.ds(pl.multiple_of(i * ROWS, ROWS), ROWS), :] = block
 
@@ -284,26 +312,57 @@
             def _():
                 output(n, i - 1).start()
 
+        @pl.loop(0, GROUP // 2)
+        def _(pair):
+            for turn, event in events:
+                pl.when(pair == turn)(event)
+            block_step(2 * pair, (scores_a, tops_a), (scores_b, tops_b))
+            block_step(2 * pair + 1, (scores_b, tops_b), (scores_a, tops_a))
+
         @pl.when(jnp.logical_not(holder))
         def _():
             output(n, GROUP - 1).start()
 
-    start_stage(0)
-    start_stage(1)
+    KEYS, VALUES, QUERIES = (0,), (1,), (2,)
+    depart(0)
     plan_blocks(row_index, slots, picks_ref, mask_ref)
-    arrive(0)
-    start_stage(3)
-    start_stage(2)
-    compute(0)
-    arrive(1)
-    compute(1)
+    arrive(0, KEYS)
+    depart(1, KEYS)
+    arrive(0, VALUES)
+    depart(1, VALUES)
+    arrive(0, QUERIES)
+    depart(1, QUERIES)
+    depart(3)
+    complete(0)
+
+    def during_first():
+        arrive(1, KEYS)
+        depart(2, KEYS)
+
+    compute(0, [(2, during_first)])
+    arrive(1, VALUES)
+    depart(2, VALUES)
+    arrive(1, QUERIES)
+    depart(2, QUERIES)
+    complete(1)
+
+    def during_second():
+        pl.when(holder)(lambda: arrive(3))
+
+    compute(1, [(3, during_second)])
 
     @pl.when(holder)
     def _():
-        arrive(3)
-        compute(3)
-
-    arrive(2)
+        complete(3)
+        compute(3, [(0, lambda: arrive(2, KEYS)), (2, lambda: arrive(2, VALUES))])
+
+    @pl.when(jnp.logical_not(holder))
+    def _():
+        arrive(2, KEYS)
+        arrive(2, VALUES)
+
+    arrive(2, QUERIES)
+    complete(2)
     compute(2)
 
     for n in range(HEADS):
@@ -372,6 +431,9 @@
             pltpu.VMEM((SPAN, HEAD), jnp.int32),
             pltpu.VMEM((SPAN, WINDOW), jnp.float32),
             pltpu.VMEM((ROWS, WINDOW), jnp.float32),
+            pltpu.VMEM((ROWS, WINDOW), jnp.float32),
+            pltpu.VMEM((ROWS, HEAD), jnp.float32),
+            pltpu.VMEM((ROWS, HEAD), jnp.float32),
             dma((stages, 3, GROUP)), dma((stages, 3, GROUP)), dma((stages, 3)),
             dma((stages, 3, GROUP)), dma((stages, 3, GROUP)),
             dma((stages, GROUP)), dma((stages, GROUP)),

time: 120 us -> 104 us (0.87)
  Pallas kernels: 114 us -> 98.2 us
    pallas_call x1, Pallas kernels: 114 us -> 98.2 us  [body(): pl.pallas_call(functools.partial(kernel, count), out_shape=jax.ShapeDtype...]
where the time goes in v3:
time: 104 us
  Pallas kernels  98.2 us (94%)
  local copies, waits for them, and re-layouts  3.53 us (3%)
  other arithmetic  1.82 us (2%)
    pallas_call x1, Pallas kernels, body(): pl.pallas_call(functools.partial(kernel, count), out_shape=jax.ShapeDtype...  98.2 us
    unnamed x1, local copies, waits for them, and re-layouts  2.7 us

profile of v3, /device:TPU:5, one launch (start us, length us, event | category | flops | bytes accessed | tf_op | source)
XLA Modules:
  0.0 103.6 jit_solution(11011530494556435811)
XLA Ops:
  0.0 0.7 mul.9
  0.7 0.3 reduce-window.9
  1.0 0.1 slice.13
  1.1 0.1 slice_reduce_fusion
  1.2 0.1 add_bitcast_fusion
  1.3 0.7 fusion
  2.1 0.6 reshape.25.slots
  2.7 98.2 %packed_attention.1 = bf16[64,12800]{1,0:T(8,128)(2,1)} custom-call(s32[2,9,128]{2,1,0:T(8,128)} %reshape.25.slots, bf16[256,3200]{1,0:T(8,128)(2,1)} %k_in.1, bf16[256,3200]{1,0:T(8,128)(2,1)} %v_in.1, bf16[256,3200]{1,0:T(8,128)(2,1)} %q_in.1, f32[100,128]{1,0:T(8,128)} %bitcast.6, f32[100,128]{1,0:T(8,128)} %bitcast.7), custom_call_target="tpu_custom_call" | custom-call | tf_op jit(solution)/shard_map/packed_attention/pallas_call | solution.py:420
  100.9 2.7 %copy.9 = bf16[64,12800]{1,0:T(8,128)(2,1)} copy(bf16[64,12800]{1,0:T(8,128)(2,1)} %packed_attention.1) | data formatting | bytes 3276800
  (6 shorter events, 0.1 us)
